TPU v7x, 128 devices: a whole 4x4x4 slice. The times are simulated.
128 devices in a mesh: dp: 4 (over z), expert: 32 (over x, y, core).
Axes of the slice: x: 4, y: 4, z: 4, core: 2. Of those that a mesh axis runs over, the one named last changes fastest.
Arguments:
- tokens: bfloat16 [16384, 2048], P(('dp', 'expert')), may hold values from -6 to 6
- routes: int32 [16384, 8], P(('dp', 'expert')), may hold values from 0 to 63, all different within a row; in each aligned block of 128 rows (0 to 127, 128 to 255, ...) at most 24 rows name the same one
- route_weights: float32 [16384, 8], P(('dp', 'expert')), may hold values from 0.05 to 0.3
- cotangent: bfloat16 [16384, 2048], P(('dp', 'expert')), may hold values from -6 to 6
- gate_proj: bfloat16 [64, 2048, 640], P('expert'), may hold values from -0.125 to 0.125
- up_proj: bfloat16 [64, 2048, 640], P('expert'), may hold values from -0.125 to 0.125
- down_proj: bfloat16 [64, 640, 2048], P('expert'), may hold values from -0.25 to 0.25
Outputs:
- layer_output: bfloat16 [16384, 2048], P(('dp', 'expert'))
- input_grad: bfloat16 [16384, 2048], P(('dp', 'expert'))
- route_weight_grad: float32 [16384, 8], P(('dp', 'expert'))
- gate_grad: float32 [2048, 64, 640], P('dp', 'expert')
- up_grad: float32 [2048, 64, 640], P('dp', 'expert')
- down_grad: float32 [2048, 64, 640], P('dp', 'expert')
Inputs may be any that keep to these rules, and one draw needn't show every extreme that they name: `routes`: each row names 8 different experts. Among the 128 rows of one device, no expert is named by more than 24 rows, a bound that some block reaches.
All inputs are finite; a program needn't handle non-finite values.
Results may differ from a plain program's by a relative error of at most 0.0095.
Values may be sent and summed in bfloat16 or wider, within the bound.
A program may use at most 192 MiB of HBM per device.

v0:
```python
import jax
import jax.numpy as jnp
from jax import lax
from jax.sharding import PartitionSpec as P


def swish_parts(gate_pre):
    sig_value = jax.nn.sigmoid(gate_pre)
    return (gate_pre * sig_value, sig_value * (1.0 + gate_pre * (1.0 - sig_value)))


def project_in(arrived, gate_proj, up_proj):
    gate_pre = jnp.einsum("secd,edh->sech", arrived, gate_proj, preferred_element_type=jnp.float32)
    up_pre = jnp.einsum("secd,edh->sech", arrived, up_proj, preferred_element_type=jnp.float32)
    return (gate_pre, up_pre)


def project_out(gate_pre, up_pre, down_proj):
    swish = swish_parts(gate_pre)[0]
    hidden = (swish * up_pre).astype(jnp.bfloat16)
    return jnp.einsum(
        "sech,ehd->secd", hidden, down_proj, preferred_element_type=jnp.float32
    ).astype(jnp.bfloat16)


def three_terms(feat_rows, cot_rows, d_gate, d_up, hidden):
    return jnp.stack(
        [
            jnp.einsum("secd,sech->deh", feat_rows, d_gate, preferred_element_type=jnp.float32),
            jnp.einsum("secd,sech->deh", feat_rows, d_up, preferred_element_type=jnp.float32),
            jnp.einsum("secd,sech->deh", cot_rows, hidden, preferred_element_type=jnp.float32),
        ],
        axis=1,
    )


def on_device(tokens, routes, route_weights, cotangent, gate_proj, up_proj, down_proj):
    tok_dev, model_width = tokens.shape
    top_count = routes.shape[1]
    exp_dev = gate_proj.shape[0]
    groups = lax.axis_size("expert")
    experts = exp_dev * groups
    capacity = 3 * tok_dev * top_count // (2 * experts)
    n_routes = tok_dev * top_count
    flat_expert = routes.reshape(-1)
    onehot = (flat_expert[:, None] == jnp.arange(experts, dtype=jnp.int32)[None, :]).astype(
        jnp.int32
    )
    before = jnp.cumsum(onehot, axis=0) - onehot
    position = jnp.sum(before * onehot, axis=1)
    slot_index = flat_expert * capacity + position
    slot_source = (
        jnp.full((experts * capacity,), n_routes, jnp.int32)
        .at[slot_index]
        .set(jnp.arange(n_routes, dtype=jnp.int32))
    )
    token_of = slot_source // top_count
    padded_x = jnp.concatenate([tokens, jnp.zeros((1, model_width), tokens.dtype)], 0)
    outgoing = padded_x[token_of].reshape(groups, exp_dev, capacity, model_width)
    arrived = lax.all_to_all(outgoing, "expert", split_axis=0, concat_axis=0, tiled=True)
    gate_pre, up_pre = project_in(arrived, gate_proj, up_proj)
    expert_out, arrived, gate_pre, up_pre = (
        project_out(gate_pre, up_pre, down_proj),
        arrived,
        gate_pre,
        up_pre,
    )
    returned = lax.all_to_all(expert_out, "expert", split_axis=0, concat_axis=0, tiled=True)
    route_out = returned.reshape(experts * capacity, model_width)[slot_index].reshape(
        tok_dev, top_count, model_width
    )
    layer_output = jnp.sum(
        route_out.astype(jnp.float32) * route_weights[:, :, None], axis=1
    ).astype(jnp.bfloat16)
    route_weight_grad = jnp.einsum(
        "tkd,td->tk", route_out, cotangent, preferred_element_type=jnp.float32
    )
    route_cot = (route_weights[:, :, None] * cotangent[:, None, :].astype(jnp.float32)).astype(
        jnp.bfloat16
    )
    padded_cot = jnp.concatenate(
        [route_cot.reshape(n_routes, model_width), jnp.zeros((1, model_width), jnp.bfloat16)], 0
    )
    cot_out = padded_cot[slot_source].reshape(groups, exp_dev, capacity, model_width)
    arrived_cot = lax.all_to_all(cot_out, "expert", split_axis=0, concat_axis=0, tiled=True)
    swish, d_swish = swish_parts(gate_pre)
    hidden = (swish * up_pre).astype(jnp.bfloat16)
    d_hidden = jnp.einsum(
        "secd,ehd->sech", arrived_cot, down_proj, preferred_element_type=jnp.float32
    )
    d_gate = (d_hidden * up_pre * d_swish).astype(jnp.bfloat16)
    d_up = (d_hidden * swish).astype(jnp.bfloat16)
    route_dx = (
        jnp.einsum("sech,edh->secd", d_gate, gate_proj, preferred_element_type=jnp.float32)
        + jnp.einsum("sech,edh->secd", d_up, up_proj, preferred_element_type=jnp.float32)
    ).astype(jnp.bfloat16)
    dx_back = lax.all_to_all(route_dx, "expert", split_axis=0, concat_axis=0, tiled=True)
    token_dx = dx_back.reshape(experts * capacity, model_width)[slot_index].reshape(
        tok_dev, top_count, model_width
    )
    input_grad = jnp.sum(token_dx.astype(jnp.float32), axis=1).astype(jnp.bfloat16)
    full_terms = three_terms(arrived, arrived_cot, d_gate, d_up, hidden)
    shares = lax.psum_scatter(
        full_terms.astype(jnp.bfloat16), "dp", scatter_dimension=0, tiled=True
    ).astype(jnp.float32)
    return (layer_output, input_grad, route_weight_grad, shares[:, 0], shares[:, 1], shares[:, 2])


def solution(mesh):
    placed = (
        P(("dp", "expert"), None),
        P(("dp", "expert"), None),
        P(("dp", "expert"), None),
        P(("dp", "expert"), None),
        P("expert", None, None),
        P("expert", None, None),
        P("expert", None, None),
    )
    return jax.shard_map(
        on_device,
        mesh=mesh,
        in_specs=placed,
        out_specs=(
            P(("dp", "expert"), None),
            P(("dp", "expert"), None),
            P(("dp", "expert"), None),
            P("dp", "expert", None),
            P("dp", "expert", None),
            P("dp", "expert", None),
        ),
        check_vma=False,
    )
```

profile of v0, /device:TPU:8, one launch (start us, length us, event | category | flops | bytes accessed | tf_op | source)
XLA Modules:
  0.0 514.0 jit_solution(16498976671464321603)
XLA Ops:
  7.2 0.7 broadcast_multiply_fusion
  7.9 0.8 copy.44
  8.6 0.1 eq.29
  8.7 0.1 eq.25
  8.8 0.1 copy.43
  8.9 0.1 mul.70
  9.1 18.0 %reduce-window.6 = s32[64,8,128]{2,1,0:T(8,128)S(1)} reduce-window(s32[64,8,128]{2,1,0:T(8,128)S(1)} %fusion.45, s32[]{:T(128)} %constant.30.clone.1), window={size=1x1x128 pad=0_0x0_0x127_0}, to_apply=%region_0.0 | reduce-window | flops 8323072 | bytes 524292 | tf_op jit(solution)/shard_map/reduce-window
  27.1 0.1 slice.28
  27.2 0.1 copy.46
  27.4 0.1 copy.47
  27.5 0.1 broadcast_add_fusion
  27.6 0.1 fusion.44
  27.7 0.0 copy-start.5
  27.7 4.3 scatter_custom_fusion
  32.1 0.0 copy-done.5
  32.1 1.1 concatenate.6
  33.2 7.1 %gather_fusion = bf16[1536,2048]{1,0:T(8,128)(2,1)} fusion(bf16[129,2048]{1,0:T(8,128)(2,1)S(1)} %concatenate.6, s32[2048]{0:T(1024)S(1)} %get-tuple-element.33), kind=kCustom, calls=%fused_computation | custom fusion | bytes 12589056 | tf_op jit(solution)/shard_map/gather | solution.py:59
  40.3 7.7 %all-to-all-start = ((bf16[32,2,24,2048]{3,2,1,0:T(8,128)(2,1)}), bf16[32,2,24,2048]{3,2,1,0:T(8,128)(2,1)}, u32[]{:S(2)}, u32[]{:S(2)}) async-start(bf16[32,2,24,2048]{3,2,1,0:T(8,128)(2,1)} %bitcast.145), calls=%async_computation | async-start | bytes 12582912 | tf_op jit(solution)/shard_map/all_to_all | solution.py:60
  48.0 0.0 copy-done.7
  48.0 0.1 copy.51
  48.1 0.1 mul.76
  48.2 0.0 copy-done.3
  48.2 0.1 convert_element_type.56
  48.4 0.9 fusion
  49.3 2.3 concatenate.7
  51.6 15.5 %gather_fusion.2 = bf16[1536,2048]{1,0:T(8,128)(2,1)} fusion(bf16[1025,2048]{1,0:T(8,128)(2,1)} %concatenate.7, s32[2048]{0:T(1024)S(1)} %get-tuple-element.32), kind=kCustom, calls=%fused_computation.2 | custom fusion | bytes 12589056 | tf_op jit(solution)/shard_map/gather | solution.py:84
  67.1 69.4 %all-to-all-done = bf16[32,2,24,2048]{3,2,1,0:T(8,128)(2,1)} async-done(((bf16[32,2,24,2048]{3,2,1,0:T(8,128)(2,1)}), bf16[32,2,24,2048]{3,2,1,0:T(8,128)(2,1)}, u32[]{:S(2)}, u32[]{:S(2)}) %all-to-all-start) | async-done | bytes 6291488 | tf_op jit(solution)/shard_map/all_to_all | solution.py:60
  136.5 4.7 all-to-all-start.2
  141.2 0.5 reduce-scatter.2.cloned.1.call-start
  141.7 10.0 %fusion.11 = f32[2,32,24,640]{3,2,1,0:T(8,128)} fusion(bf16[2,2048,640]{2,1,0:T(8,128)(2,1)} %param.12, bf16[32,2,24,2048]{3,2,1,0:T(8,128)(2,1)} %all-to-all-done), kind=kOutput, calls=%fused_computation.24 | convolution fusion | flops 4026531840 | bytes 15466496 | tf_op jit(solution)/shard_map/secd,edh->sech/dot_general | solution.py:14
  151.7 10.0 %fusion.15 = f32[2,32,24,640]{3,2,1,0:T(8,128)} fusion(bf16[2,2048,640]{2,1,0:T(8,128)(2,1)} %param.11, bf16[32,2,24,2048]{3,2,1,0:T(8,128)(2,1)} %all-to-all-done), kind=kOutput, calls=%fused_computation.28 | convolution fusion | flops 4026531840 | bytes 15466496 | tf_op jit(solution)/shard_map/secd,edh->sech/dot_general | solution.py:13
  161.7 66.2 %all-to-all-done.2 = bf16[32,2,24,2048]{3,2,1,0:T(8,128)(2,1)} async-done(((bf16[32,2,24,2048]{3,2,1,0:T(8,128)(2,1)}), bf16[32,2,24,2048]{3,2,1,0:T(8,128)(2,1)}, u32[]{:S(2)}, u32[]{:S(2)}) %all-to-all-start.2) | async-done | bytes 6291488 | tf_op jit(solution)/shard_map/all_to_all | solution.py:85
  227.9 11.1 %fusion.33 = (bf16[32,2,24,640]{3,2,0,1:T(8,128)(2,1)S(1)}, bf16[32,2,24,640]{3,2,0,1:T(8,128)(2,1)S(1)}, bf16[32,2,24,640]{3,2,0,1:T(8,128)(2,1)S(1)}) fusion(f32[2,32,24,640]{3,2,1,0:T(8,128)} %fusion.11, f32[2,32,24,640]{3,2,1,0:T(8,128)} %fusion.15, bf16[2,640,2048]{2,1,0:T(8,128)(2,1)} %param.13, bf16[32,2,24,2048]{3,2,1,0:T(8,128)(2,1)} %all-to-all-done.2), kind=kOutput, calls=%fused_computation.43 | convolution fusion | flops 4041277440 | bytes 25296896 | tf_op jit(solution)/shard_map/secd,ehd->sech/dot_general | solution.py:88
  239.1 0.0 copy-start.8
  239.1 0.0 copy-start.9
  239.1 8.6 %fusion.8 = bf16[2048,1,2,640]{0,3,2,1:T(8,128)(2,1)S(1)} fusion(bf16[32,2,24,640]{3,2,0,1:T(8,128)(2,1)S(1)} %get-tuple-element.28, bf16[32,2,24,2048]{3,2,1,0:T(8,128)(2,1)} %all-to-all-done.2), kind=kOutput, calls=%fused_computation.21 | convolution fusion | flops 4029153280 | bytes 13500416 | tf_op jit(solution)/shard_map/secd,sech->deh/dot_general | solution.py:31
  247.7 7.1 %fusion.6 = bf16[2048,1,2,640]{0,3,2,1:T(8,128)(2,1)S(1)} fusion(bf16[32,2,24,640]{3,2,0,1:T(8,128)(2,1)S(1)} %get-tuple-element.27, bf16[32,2,24,2048]{3,2,1,0:T(8,128)(2,1)} %all-to-all-done), kind=kOutput, calls=%fused_computation.19 | convolution fusion | flops 4029153280 | bytes 13500416 | tf_op jit(solution)/shard_map/secd,sech->deh/dot_general | solution.py:29
  254.8 7.4 %fusion.7 = bf16[2048,1,2,640]{0,3,2,1:T(8,128)(2,1)S(1)} fusion(bf16[32,2,24,640]{3,2,0,1:T(8,128)(2,1)S(1)} %get-tuple-element.29, bf16[32,2,24,2048]{3,2,1,0:T(8,128)(2,1)} %all-to-all-done), kind=kOutput, calls=%fused_computation.20 | convolution fusion | flops 4029153280 | bytes 13500416 | tf_op jit(solution)/shard_map/secd,sech->deh/dot_general | solution.py:30
  262.2 6.8 %pad_maximum_fusion = bf16[2048,3,2,640]{0,3,2,1:T(8,128)(2,1)} fusion(bf16[2048,1,2,640]{0,3,2,1:T(8,128)(2,1)S(1)} %fusion.8, bf16[2048,1,2,640]{0,3,2,1:T(8,128)(2,1)S(1)} %fusion.7, bf16[2048,1,2,640]{0,3,2,1:T(8,128)(2,1)S(1)} %fusion.6), kind=kLoop, calls=%fused_computation.5 | loop fusion | flops 15728640 | bytes 31457280 | tf_op jit(solution)/shard_map/stack | solution.py:27
  269.0 0.0 reduce-scatter.2.cloned.1.call-update
  269.0 7.8 %convert_bitcast_fusion = bf16[32,2,24,2048]{3,2,0,1:T(8,128)(2,1)S(1)} fusion(bf16[32,2,24,640]{3,2,0,1:T(8,128)(2,1)S(1)} %get-tuple-element.28, bf16[2,640,2048]{2,1,0:T(8,128)(2,1)} %param.13), kind=kOutput, calls=%fused_computation.14 | convolution fusion | flops 4029677568 | bytes 13500416 | tf_op jit(solution)/shard_map/sech,ehd->secd/dot_general | solution.py:21
  276.8 3.2 copy.50
  280.0 4.8 all-to-all-start.1
  284.8 0.0 slice-start.1
  284.8 11.2 %fusion.9 = f32[2,32,24,2048]{3,2,1,0:T(8,128)} fusion(bf16[32,2,24,640]{3,2,0,1:T(8,128)(2,1)} %copy-done.9, bf16[2,2048,640]{2,1,0:T(8,128)(2,1)} %param.12), kind=kOutput, calls=%fused_computation.22 | convolution fusion | flops 4026531840 | bytes 19791872 | tf_op jit(solution)/shard_map/sech,edh->secd/dot_general | solution.py:95
  296.0 0.0 slice-done.1
  296.0 8.9 %fusion.1 = bf16[32,2,24,2048]{3,2,0,1:T(8,128)(2,1)S(1)} fusion(f32[2,32,24,2048]{3,2,1,0:T(8,128)} %fusion.9, bf16[32,2,24,640]{3,2,0,1:T(8,128)(2,1)} %copy-done.8, bf16[2,2048,640]{2,1,0:T(8,128)(2,1)S(1)} %bitcast.155), kind=kOutput, calls=%fused_computation.13 | convolution fusion | flops 4032823296 | bytes 26083328 | tf_op jit(solution)/shard_map/sech,edh->secd/dot_general | solution.py:94
  305.0 3.8 copy.54
  308.8 62.8 %all-to-all-done.1 = bf16[32,2,24,2048]{3,2,1,0:T(8,128)(2,1)} async-done(((bf16[32,2,24,2048]{3,2,1,0:T(8,128)(2,1)}), bf16[32,2,24,2048]{3,2,1,0:T(8,128)(2,1)}, u32[]{:S(2)}, u32[]{:S(2)}) %all-to-all-start.1) | async-done | bytes 6291488 | tf_op jit(solution)/shard_map/all_to_all | solution.py:68
  371.6 4.9 all-to-all-start.3
  376.6 0.0 copy-start.4
  376.6 12.6 %gather_fusion.1 = bf16[1024,2048]{1,0:T(8,128)(2,1)} fusion(bf16[1536,2048]{1,0:T(8,128)(2,1)} %bitcast.14, s32[1024]{0:T(1024)S(1)} %broadcast_clamp_fusion), kind=kCustom, calls=%fused_computation.1 | custom fusion | bytes 8392704 | tf_op jit(solution)/shard_map/gather | solution.py:69
  389.2 4.9 fusion.24
  394.1 0.7 copy.65
  394.8 68.2 %all-to-all-done.3 = bf16[32,2,24,2048]{3,2,1,0:T(8,128)(2,1)} async-done(((bf16[32,2,24,2048]{3,2,1,0:T(8,128)(2,1)}), bf16[32,2,24,2048]{3,2,1,0:T(8,128)(2,1)}, u32[]{:S(2)}, u32[]{:S(2)}) %all-to-all-start.3) | async-done | bytes 6291488 | tf_op jit(solution)/shard_map/all_to_all | solution.py:97
  462.9 12.5 %gather_fusion.3 = bf16[1024,2048]{1,0:T(8,128)(2,1)} fusion(bf16[1536,2048]{1,0:T(8,128)(2,1)} %bitcast.23, s32[1024]{0:T(1024)S(1)} %broadcast_clamp_fusion), kind=kCustom, calls=%fused_computation.3 | custom fusion | bytes 8392704 | tf_op jit(solution)/shard_map/gather | solution.py:98
  475.4 6.0 %bitcast_reduce_fusion = bf16[128,2048]{1,0:T(8,128)(2,1)} fusion(bf16[1024,2048]{1,0:T(8,128)(2,1)} %gather_fusion.3), kind=kLoop, calls=%fused_computation.33 | loop fusion | flops 1835008 | bytes 4718592 | tf_op jit(solution)/shard_map/reduce_sum | solution.py:101
  481.4 0.0 copy-done.2
  481.5 5.2 %multiply_reduce_fusion = bf16[128,2048]{1,0:T(8,128)(2,1)} fusion(bf16[1024,2048]{1,0:T(8,128)(2,1)S(1)} %copy-done, f32[128,8]{1,0:T(8,128)S(1)} %copy-done.2), kind=kLoop, calls=%fused_computation.12 | loop fusion | flops 6029312 | bytes 4722688 | tf_op jit(solution)/shard_map/reduce_sum | solution.py:72
  486.6 3.2 convert_element_type.62
  489.8 3.6 slice_bitcast_fusion
  493.4 5.1 copy.60
  498.5 5.1 copy.59
  503.6 3.1 copy.58
  (24 shorter events, 0.1 us)
Async XLA Ops:
  27.7 4.4 copy-start.5
  40.3 7.7 %copy-start.7 = (f32[128,8]{0,1:T(8,128)S(1)}, f32[128,8]{0,1:T(8,128)}, u32[]{:S(2)}) copy-start(f32[128,8]{0,1:T(8,128)} %param.9) | copy-start | bytes 12292
  40.3 7.9 %copy-start.3 = (bf16[128,2048]{1,0:T(8,128)(2,1)S(1)}, bf16[128,2048]{1,0:T(8,128)(2,1)}, u32[]{:S(2)}) copy-start(bf16[128,2048]{1,0:T(8,128)(2,1)} %param.10) | copy-start | bytes 1572868
  40.3 96.2 %all-to-all-start = ((bf16[32,2,24,2048]{3,2,1,0:T(8,128)(2,1)}), bf16[32,2,24,2048]{3,2,1,0:T(8,128)(2,1)}, u32[]{:S(2)}, u32[]{:S(2)}) async-start(bf16[32,2,24,2048]{3,2,1,0:T(8,128)(2,1)} %bitcast.145), calls=%async_computation | async-start | bytes 12582912 | tf_op jit(solution)/shard_map/all_to_all | solution.py:60
  48.1 3.5 copy-start.1
  136.5 91.4 %all-to-all-start.2 = ((bf16[32,2,24,2048]{3,2,1,0:T(8,128)(2,1)}), bf16[32,2,24,2048]{3,2,1,0:T(8,128)(2,1)}, u32[]{:S(2)}, u32[]{:S(2)}) async-start(bf16[32,2,24,2048]{3,2,1,0:T(8,128)(2,1)} %bitcast.146), calls=%async_computation.2 | async-start | bytes 12582912 | tf_op jit(solution)/shard_map/all_to_all | solution.py:85
  141.2 345.4 %reduce-scatter.2.cloned.1.call-start = ((), (), s32[]{:S(2)}) async-start(), calls=%async_computation.5 | async-start | bytes 19660800 | tf_op jit(solution)/shard_map/reduce_scatter | solution.py:103
  239.1 8.6 %copy-start.8 = (bf16[32,2,24,640]{3,2,0,1:T(8,128)(2,1)}, bf16[32,2,24,640]{3,2,0,1:T(8,128)(2,1)S(1)}, u32[]{:S(2)}) copy-start(bf16[32,2,24,640]{3,2,0,1:T(8,128)(2,1)S(1)} %get-tuple-element.27) | copy-start | bytes 5898244
  239.1 15.7 %copy-start.9 = (bf16[32,2,24,640]{3,2,0,1:T(8,128)(2,1)}, bf16[32,2,24,640]{3,2,0,1:T(8,128)(2,1)S(1)}, u32[]{:S(2)}) copy-start(bf16[32,2,24,640]{3,2,0,1:T(8,128)(2,1)S(1)} %get-tuple-element.29) | copy-start | bytes 5898244
  280.0 16.1 %slice-start = ((s8[5242880]{0:T(1024)(128)(4,1)}), s8[1048576]{0:T(1024)(128)(4,1)S(1)}, s32[]{:S(2)}) async-start(s8[5242880]{0:T(1024)(128)(4,1)} %bitcast.154), calls=%async_computation.6 | async-start | bytes 2097152
  280.0 91.6 %all-to-all-start.1 = ((bf16[32,2,24,2048]{3,2,1,0:T(8,128)(2,1)}), bf16[32,2,24,2048]{3,2,1,0:T(8,128)(2,1)}, u32[]{:S(2)}, u32[]{:S(2)}) async-start(bf16[32,2,24,2048]{3,2,1,0:T(8,128)(2,1)} %copy.50), calls=%async_computation.1 | async-start | bytes 12582912 | tf_op jit(solution)/shard_map/all_to_all | solution.py:68
  284.8 11.2 %slice-start.1 = ((s8[5242880]{0:T(1024)(128)(4,1)}), s8[4194304]{0:T(1024)(128)(4,1)S(1)}, s32[]{:S(2)}) async-start(s8[5242880]{0:T(1024)(128)(4,1)} %bitcast.154), calls=%async_computation.7 | async-start | bytes 8388608
  308.8 67.8 %copy-start.6 = (s32[1024,1]{0,1:T(1,128)S(1)}, s32[1024,1]{0,1:T(1,128)}, u32[]{:S(2)}) copy-start(s32[1024,1]{0,1:T(1,128)} %copy-done.5) | copy-start | bytes 12292
  371.6 91.4 %all-to-all-start.3 = ((bf16[32,2,24,2048]{3,2,1,0:T(8,128)(2,1)}), bf16[32,2,24,2048]{3,2,1,0:T(8,128)(2,1)}, u32[]{:S(2)}, u32[]{:S(2)}) async-start(bf16[32,2,24,2048]{3,2,1,0:T(8,128)(2,1)} %copy.54), calls=%async_computation.3 | async-start | bytes 12582912 | tf_op jit(solution)/shard_map/all_to_all | solution.py:97
  376.6 12.6 %copy-start.4 = (bf16[128,2048]{1,0:T(8,128)(2,1)S(1)}, bf16[128,2048]{1,0:T(8,128)(2,1)}, u32[]{:S(2)}) copy-start(bf16[128,2048]{1,0:T(8,128)(2,1)} %param.10) | copy-start | bytes 1572868
  462.9 18.5 %copy-start.2 = (f32[128,8]{1,0:T(8,128)S(1)}, f32[128,8]{1,0:T(8,128)}, u32[]{:S(2)}) copy-start(f32[128,8]{1,0:T(8,128)} %copy-done.1) | copy-start | bytes 12292
  475.4 6.0 %copy-start = (bf16[1024,2048]{1,0:T(8,128)(2,1)S(1)}, bf16[1024,2048]{1,0:T(8,128)(2,1)}, u32[]{:S(2)}) copy-start(bf16[1024,2048]{1,0:T(8,128)(2,1)} %gather_fusion.1) | copy-start | bytes 12582916
Sparse Core Ops, SparseCore 0:
  269.1 138.4 reduce-scatter.1
where the time goes:
time: 521 us; the launch traced here: 514 us
  waiting for transfers between devices  267 us (51%)
  matrix products  86.9 us (17%)
  local copies, waits for them, and re-layouts  81.8 us (16%)
  other arithmetic  41.2 us (8%)
  starting transfers between devices  22.7 us (4%)
  between operations  14.8 us (3%)
    all_to_all x1, waiting for transfers between devices, on_device(): lax.all_to_all(outgoing, 'expert', split_axis=0, concat_axis=0, tiled=True)  69.4 us
    all_to_all x1, waiting for transfers between devices, on_device(): lax.all_to_all(route_dx, 'expert', split_axis=0, concat_axis=0, tiled=True)  68.2 us
    all_to_all x1, waiting for transfers between devices, on_device(): lax.all_to_all(cot_out, 'expert', split_axis=0, concat_axis=0, tiled=True)  66.2 us
    all_to_all x1, waiting for transfers between devices, on_device(): lax.all_to_all(expert_out, 'expert', split_axis=0, concat_axis=0, tiled=T...  62.8 us
    another operation x3, other arithmetic  18.2 us
    gather x1, local copies, waits for them, and re-layouts, on_device(): padded_cot[slot_source].reshape(groups, exp_dev, capacity, model_width)  15.5 us
    unnamed x29, local copies, waits for them, and re-layouts  14.3 us
    gather x1, local copies, waits for them, and re-layouts, on_device(): returned.reshape(experts * capacity, model_width)[slot_index]  12.6 us
  transfers between devices with their start and end apart: 5, of which 4 were waited for; matrix products, arithmetic and copies ran while one was open for 23% of the time, Pallas kernels for 0%

commit v1 on v0

v1 whole, which is shorter than its diff:
```python
import jax
import jax.numpy as jnp
from jax import lax
from jax.experimental import pallas as pl
from jax.experimental.pallas import tpu as pltpu
from jax.sharding import PartitionSpec as P

MESH = pl.DeviceIdType.MESH
BF = jnp.bfloat16
F32 = jnp.float32
SIDE = 4
TOK = 128
HALF = 64
SUB = 32
CAP = 24
META = 128


def _place():
    me = lax.axis_index("expert")
    return lax.axis_index("dp"), me // 8, (me // 2) % 4, me % 2


def _at(x, y, c):
    return ((x + 8) % 4) * 8 + ((y + 8) % 4) * 2 + c


def _greet(peers):
    barrier = pltpu.get_barrier_semaphore()
    for peer in peers:
        pl.semaphore_signal(barrier, inc=1, device_id=peer, device_id_type=MESH)
    pl.semaphore_wait(barrier, len(peers))


def _shift(h, x, y, o1, o2, c):
    return _at(x + o1, y + o2, c) if h == 0 else _at(x + o2, y + o1, c)


def _gather_kernel(blk, out, ssem, rsem, lsem):
    z, x, y, c = _place()
    sib = _at(x, y, 1 - c)
    _greet(
        [(z, _at(x + 1, y, c)), (z, _at(x - 1, y, c)), (z, _at(x, y + 1, c)), (z, _at(x, y - 1, c)), (z, sib)]
    )
    mine = _at(x, y, c)
    own = pltpu.make_async_copy(blk, out.at[mine], lsem)
    own.start()
    sends, keys = [], {}

    def key(*k):
        return keys.setdefault(k, len(keys))

    def send(slot, row, n, to, k):
        src = blk.at[pl.ds(row, n)] if slot is None else out.at[slot, pl.ds(row, n)]
        cp = pltpu.make_async_remote_copy(
            src_ref=src,
            dst_ref=out.at[mine if slot is None else slot, pl.ds(row, n)],
            send_sem=ssem.at[len(sends)],
            recv_sem=rsem.at[k],
            device_id=(z, to),
            device_id_type=MESH,
        )
        cp.start()
        sends.append(cp)

    def landed(slot, row, n, k):
        view = out.at[slot, pl.ds(row, n)]
        pltpu.make_async_remote_copy(
            src_ref=view,
            dst_ref=view,
            send_sem=ssem.at[0],
            recv_sem=rsem.at[k],
            device_id=(z, sib),
            device_id_type=MESH,
        ).wait_recv()

    def line(h, o1, slot):
        send(slot, h * HALF, HALF, _shift(h, x, y, 0, 1, c), key(h, "G+", o1))
        send(slot, h * HALF, HALF, _shift(h, x, y, 0, -1, c), key(h, "G-", o1))

    def aside(h, o1, o2, slot):
        send(slot, h * HALF, HALF, sib, key(h, "S", o1, o2))

    def start(h):
        send(None, h * HALF, HALF, _shift(h, x, y, 1, 0, c), key(h, "F+"))
        send(None, h * HALF, HALF, _shift(h, x, y, -1, 0, c), key(h, "F-"))
        line(h, 0, None)
        aside(h, 0, 0, None)

    def first(h, up):
        o = -1 if up else 1
        slot = _shift(h, x, y, o, 0, c)
        landed(slot, h * HALF, HALF, key(h, "F+" if up else "F-"))
        row = h * HALF + (0 if up else SUB)
        send(slot, row, SUB, _shift(h, x, y, 1 if up else -1, 0, c), key(h, "FF+" if up else "FF-"))
        line(h, o, slot)
        aside(h, o, 0, slot)

    def far(h):
        slot = _shift(h, x, y, 2, 0, c)
        landed(slot, h * HALF, SUB, key(h, "FF+"))
        landed(slot, h * HALF + SUB, SUB, key(h, "FF-"))
        line(h, 2, slot)
        aside(h, 2, 0, slot)

    def second(h, o1, up):
        o = -1 if up else 1
        slot = _shift(h, x, y, o1, o, c)
        landed(slot, h * HALF, HALF, key(h, "G+" if up else "G-", o1))
        row = h * HALF + (0 if up else SUB)
        send(slot, row, SUB, _shift(h, x, y, 0, 1 if up else -1, c), key(h, "GF+" if up else "GF-", o1))
        aside(h, o1, o, slot)

    def corner(h, o1):
        slot = _shift(h, x, y, o1, 2, c)
        landed(slot, h * HALF, SUB, key(h, "GF+", o1))
        landed(slot, h * HALF + SUB, SUB, key(h, "GF-", o1))
        aside(h, o1, 2, slot)

    both = (0, 1)
    for h in both:
        start(h)
    for up in (True, False):
        for h in both:
            first(h, up)
    for up in (True, False):
        for h in both:
            second(h, 0, up)
    for h in both:
        far(h)
    for o1 in (-1, 1):
        for up in (True, False):
            for h in both:
                second(h, o1, up)
    for h in both:
        corner(h, 0)
    for up in (True, False):
        for h in both:
            second(h, 2, up)
    for o1 in (-1, 1, 2):
        for h in both:
            corner(h, o1)
    for o2 in (0, -1, 1, 2):
        for o1 in (0, -1, 1, 2):
            for h in both:
                landed(_shift(h, x, y, o1, o2, 1 - c), h * HALF, HALF, key(h, "S", o1, o2))
    for cp in sends:
        cp.wait_send()
    own.wait()


def _gather(blk):
    width = blk.shape[1]
    return pl.pallas_call(
        _gather_kernel,
        out_shape=jax.ShapeDtypeStruct((32, TOK, width), BF),
        in_specs=[pl.BlockSpec(memory_space=pltpu.VMEM)],
        out_specs=pl.BlockSpec(memory_space=pl.ANY),
        scratch_shapes=[
            pltpu.SemaphoreType.DMA((72,)),
            pltpu.SemaphoreType.DMA((72,)),
            pltpu.SemaphoreType.DMA,
        ],
        compiler_params=pltpu.CompilerParams(collective_id=0, has_side_effects=True),
        name="plane_gather",
    )(blk)


def _add(dst, src, n):
    @pl.loop(0, n // 16)
    def _(i):
        rows = pl.ds(pl.multiple_of(i * 16, 16), 16)
        dst[rows, :] = (dst[rows, :].astype(F32) + src[rows, :].astype(F32)).astype(BF)


def _add3(dst, own, one, two, n):
    @pl.loop(0, n // 16)
    def _(i):
        rows = pl.ds(pl.multiple_of(i * 16, 16), 16)
        total = own[rows, :].astype(F32) + one[rows, :].astype(F32) + two[rows, :].astype(F32)
        dst[rows, :] = total.astype(dst.dtype)


def _reduce_kernel(
    part, gg, ug, dg, out, go, uo, do, aside,
    T, sb, ra, rb, r2a, r2b, za, zt, zf, zown, zout,
    ssem, rsem, tsem, bsem, zsem, osem, wsem,
):
    z, x, y, c = _place()
    sib = (z, _at(x, y, 1 - c))
    zup, zdn = ((z + 1) % 4, _at(x, y, c)), ((z + 3) % 4, _at(x, y, c))
    _greet(
        [(z, _at(x + 1, y, c)), (z, _at(x - 1, y, c)), (z, _at(x, y + 1, c)), (z, _at(x, y - 1, c)), sib, zup, zdn]
    )
    sends, keys = [], {}

    def remote(src, dst, to, *k):
        cp = pltpu.make_async_remote_copy(
            src_ref=src,
            dst_ref=dst,
            send_sem=ssem.at[len(sends)],
            recv_sem=rsem.at[keys.setdefault(k, len(keys))],
            device_id=to,
            device_id_type=MESH,
        )
        cp.start()
        sends.append(cp)

    def landed(dst, *k):
        pltpu.make_async_remote_copy(
            src_ref=dst,
            dst_ref=dst,
            send_sem=ssem.at[0],
            recv_sem=rsem.at[keys[k]],
            device_id=sib,
            device_id_type=MESH,
        ).wait_recv()

    lo, hi, full = pl.ds(0, SUB), pl.ds(SUB, SUB), pl.ds(0, HALF)
    both = (0, 1)
    obs, oas = (2, 1, 3, 0), (2, 1, 3, 0)
    order = [(h, ob, oa) for ob in obs for oa in oas for h in both]

    def ax(h, o):
        return (z, _shift(1 - h, x, y, o, 0, c))

    def bx(h, o):
        return (z, _shift(h, x, y, o, 0, c))

    def slot(h, ob, oa, core):
        return _shift(h, x, y, ob, oa, core)

    grads, couts = (gg, ug, dg), (go, uo, do)
    quads = [(k, e) for k in range(3) for e in range(2)]
    zl, zh = pl.ds(0, 256), pl.ds(256, 256)
    zp, zm, zq = (z + 1) % 4, (z + 3) % 4, (z + 2) % 4

    for q, (k, e) in enumerate(quads):
        remote(grads[k].at[e, zq, zl], za.at[q, 0], zup, "za", q, 0)
        remote(grads[k].at[e, zq, zh], za.at[q, 1], zdn, "za", q, 1)

    tcopies = {}
    for i, (h, ob, oa) in enumerate(order):
        rows = pl.ds(h * HALF, HALF)
        k = ob * 4 + oa
        remote(part.at[slot(h, ob, oa, 1 - c), rows], aside.at[h, k], sib, "s", h, ob, oa)
        cp = pltpu.make_async_copy(part.at[slot(h, ob, oa, c), rows], T.at[h, k], tsem.at[i])
        cp.start()
        tcopies[h, ob, oa] = cp
    zcopies = []
    for q, (k, e) in enumerate(quads):
        remote(grads[k].at[e, zp, zh], zf.at[q, 0, zh], zup, "zd", q, 0)
        remote(grads[k].at[e, zm, zl], zf.at[q, 1, zl], zdn, "zd", q, 1)
        pair = []
        for d, (where, rows) in enumerate(((zp, zl), (zm, zh))):
            cp = pltpu.make_async_copy(grads[k].at[e, where, rows], zt.at[q, d], zsem.at[q * 2 + d])
            cp.start()
            pair.append(cp)
        zcopies.append(pair)

    loads = {}

    def fetch(i):
        h, ob, oa = order[i]
        landed(aside.at[h, ob * 4 + oa], "s", h, ob, oa)
        cp = pltpu.make_async_copy(aside.at[h, ob * 4 + oa], sb.at[i % 3], bsem.at[i % 3])
        cp.start()
        loads[i] = cp

    def one(i):
        h, ob, oa = order[i]
        if i + 1 < len(order):
            fetch(i + 1)
        tcopies[h, ob, oa].wait()
        loads[i].wait()
        t = T.at[h, ob * 4 + oa]
        _add(t, sb.at[i % 3], HALF)
        if oa == 2:
            remote(t.at[lo], ra.at[h, ob, 0], ax(h, 1), "ra", h, ob, 0)
            remote(t.at[hi], ra.at[h, ob, 1], ax(h, -1), "ra", h, ob, 1)
        elif oa == 1:
            remote(t.at[hi], rb.at[h, ob, 0, hi], ax(h, 1), "rd", h, ob, 0)
        elif oa == 3:
            remote(t.at[lo], rb.at[h, ob, 1, lo], ax(h, -1), "rd", h, ob, 1)

    def stage1(j):
        for i in range(j * 8, j * 8 + 8):
            one(i)

    def stage2(j):
        ob = obs[j]
        for h in both:
            landed(ra.at[h, ob, 0], "ra", h, ob, 0)
            t = T.at[h, ob * 4 + 1]
            _add(t.at[lo], ra.at[h, ob, 0], SUB)
            remote(t.at[lo], rb.at[h, ob, 0, lo], ax(h, 1), "rs", h, ob, 0)
            landed(ra.at[h, ob, 1], "ra", h, ob, 1)
            t = T.at[h, ob * 4 + 3]
            _add(t.at[hi], ra.at[h, ob, 1], SUB)
            remote(t.at[hi], rb.at[h, ob, 1, hi], ax(h, -1), "rs", h, ob, 1)

    def stage3(j):
        ob = obs[j]
        for h in both:
            landed(rb.at[h, ob, 0, hi], "rd", h, ob, 0)
            landed(rb.at[h, ob, 1, lo], "rd", h, ob, 1)
            landed(rb.at[h, ob, 0, lo], "rs", h, ob, 0)
            landed(rb.at[h, ob, 1, hi], "rs", h, ob, 1)
            t = T.at[h, ob * 4]
            _add3(t, t, rb.at[h, ob, 0], rb.at[h, ob, 1], HALF)
            if ob == 2:
                remote(t.at[lo], r2a.at[h, 0], bx(h, 1), "2a", h, 0)
                remote(t.at[hi], r2a.at[h, 1], bx(h, -1), "2a", h, 1)
            elif ob == 1:
                remote(t.at[hi], r2b.at[h, 0, hi], bx(h, 1), "2d", h, 0)
            elif ob == 3:
                remote(t.at[lo], r2b.at[h, 1, lo], bx(h, -1), "2d", h, 1)

    def stage4():
        for h in both:
            landed(r2a.at[h, 0], "2a", h, 0)
            t = T.at[h, 4]
            _add(t.at[lo], r2a.at[h, 0], SUB)
            remote(t.at[lo], r2b.at[h, 0, lo], bx(h, 1), "2s", h, 0)
            landed(r2a.at[h, 1], "2a", h, 1)
            t = T.at[h, 12]
            _add(t.at[hi], r2a.at[h, 1], SUB)
            remote(t.at[hi], r2b.at[h, 1, hi], bx(h, -1), "2s", h, 1)

    def stage5():
        for h in both:
            landed(r2b.at[h, 0, hi], "2d", h, 0)
            landed(r2b.at[h, 1, lo], "2d", h, 1)
            landed(r2b.at[h, 0, lo], "2s", h, 0)
            landed(r2b.at[h, 1, hi], "2s", h, 1)
            _add3(out.at[pl.ds(h * HALF, HALF)], T.at[h, 0], r2b.at[h, 0], r2b.at[h, 1], HALF)

    def zmid(q):
        for d, (rows, to) in enumerate(((zl, zup), (zh, zdn))):
            landed(za.at[q, d], "za", q, d)
            zcopies[q][d].wait()
            _add(zt.at[q, d], za.at[q, d], 256)
            remote(zt.at[q, d], zf.at[q, d, rows], to, "zs", q, d)

    owns, writes = {}, {}

    def zload(q):
        k, e = quads[q]
        cp = pltpu.make_async_copy(grads[k].at[e, z], zown.at[q % 2], osem.at[q % 2])
        cp.start()
        owns[q] = cp

    def zend(q):
        k, e = quads[q]
        landed(zf.at[q, 0, zh], "zd", q, 0)
        landed(zf.at[q, 1, zl], "zd", q, 1)
        landed(zf.at[q, 0, zl], "zs", q, 0)
        landed(zf.at[q, 1, zh], "zs", q, 1)
        owns[q].wait()
        if q >= 2:
            writes[q - 2].wait()
        _add3(zout.at[q % 2], zown.at[q % 2], zf.at[q, 0], zf.at[q, 1], 512)
        cp = pltpu.make_async_copy(zout.at[q % 2], couts[k].at[e], wsem.at[q % 2])
        cp.start()
        writes[q] = cp
        if q + 2 < 6:
            zload(q + 2)

    zload(0)
    zload(1)
    fetch(0)
    stage1(0)
    stage1(1)
    stage2(0)
    zmid(0)
    stage1(2)
    stage2(1)
    stage3(0)
    zmid(1)
    stage1(3)
    stage2(2)
    stage3(1)
    zmid(2)
    stage2(3)
    stage3(2)
    stage4()
    zmid(3)
    stage3(3)
    zmid(4)
    stage5()
    zmid(5)
    for q in range(6):
        zend(q)
    writes[4].wait()
    writes[5].wait()
    for cp in sends:
        cp.wait_send()


def _reduce(part, gg, ug, dg):
    width = part.shape[2]
    hid = gg.shape[-1]
    grad = jax.ShapeDtypeStruct((2, 512, hid), F32)
    hbm = pl.BlockSpec(memory_space=pl.ANY)
    return pl.pallas_call(
        _reduce_kernel,
        out_shape=(
            jax.ShapeDtypeStruct((TOK, width), BF),
            grad,
            grad,
            grad,
            jax.ShapeDtypeStruct((2, 16, HALF, width), BF),
        ),
        in_specs=[hbm] * 4,
        out_specs=(pl.BlockSpec(memory_space=pltpu.VMEM), hbm, hbm, hbm, hbm),
        scratch_shapes=[
            pltpu.VMEM((2, 16, HALF, width), BF),
            pltpu.VMEM((3, HALF, width), BF),
            pltpu.VMEM((2, 4, 2, SUB, width), BF),
            pltpu.VMEM((2, 4, 2, HALF, width), BF),
            pltpu.VMEM((2, 2, SUB, width), BF),
            pltpu.VMEM((2, 2, HALF, width), BF),
            pltpu.VMEM((6, 2, 256, hid), BF),
            pltpu.VMEM((6, 2, 256, hid), BF),
            pltpu.VMEM((6, 2, 512, hid), BF),
            pltpu.VMEM((2, 512, hid), BF),
            pltpu.VMEM((2, 512, hid), F32),
            pltpu.SemaphoreType.DMA((128,)),
            pltpu.SemaphoreType.DMA((128,)),
            pltpu.SemaphoreType.DMA((32,)),
            pltpu.SemaphoreType.DMA((3,)),
            pltpu.SemaphoreType.DMA((12,)),
            pltpu.SemaphoreType.DMA((2,)),
            pltpu.SemaphoreType.DMA((2,)),
        ],
        compiler_params=pltpu.CompilerParams(
            collective_id=1, has_side_effects=True, vmem_limit_bytes=63 * 1024 * 1024
        ),
        name="plane_and_z_reduce",
    )(part, gg, ug, dg)


def _pick_kernel(all_ref, s_ref, w_ref, x_ref, c_ref):
    width = x_ref.shape[-1]
    pick = s_ref[0]
    xs = jnp.dot(pick, all_ref[0, :, :width], preferred_element_type=F32).astype(BF)
    cs = jnp.dot(pick, all_ref[0, :, width : 2 * width], preferred_element_type=F32)
    cs = (cs * w_ref[0]).astype(BF)
    for e in range(2):
        x_ref[e, 0] = xs[e * CAP : (e + 1) * CAP]
        c_ref[e, 0] = cs[e * CAP : (e + 1) * CAP]


def _pick(everything, sel, wrow, width):
    rows = jax.ShapeDtypeStruct((2, 32, CAP, width), BF)
    spec = pl.BlockSpec((2, 1, CAP, width), lambda s: (0, s, 0, 0))
    return pl.pallas_call(
        _pick_kernel,
        grid=(32,),
        out_shape=(rows, rows),
        in_specs=[
            pl.BlockSpec((1,) + everything.shape[1:], lambda s: (s, 0, 0)),
            pl.BlockSpec((1, 2 * CAP, TOK), lambda s: (s, 0, 0)),
            pl.BlockSpec((1, 2 * CAP, 1), lambda s: (s, 0, 0)),
        ],
        out_specs=(spec, spec),
        name="pick_rows",
    )(everything, sel, wrow)


def _spread_kernel(s_ref, y_ref, d_ref, r_ref, out_ref):
    width = y_ref.shape[-1]
    sel = s_ref[0]
    dims = (((0,), (0,)), ((), ()))

    def put(rows, at, n):
        out_ref[0, :, at : at + n] = lax.dot_general(sel, rows, dims, preferred_element_type=F32).astype(BF)

    put(jnp.concatenate([y_ref[0, 0], y_ref[1, 0]], 0), 0, width)
    put(jnp.concatenate([d_ref[0, 0], d_ref[1, 0]], 0), width, width)
    put(r_ref[0], 2 * width, META)


def _spread(sel, yrows, dxrows, rrows):
    width = yrows.shape[-1]
    spec = pl.BlockSpec((2, 1, CAP, width), lambda s: (0, s, 0, 0))
    full = 2 * width + META
    return pl.pallas_call(
        _spread_kernel,
        grid=(32,),
        out_shape=jax.ShapeDtypeStruct((32, TOK, full), BF),
        in_specs=[
            pl.BlockSpec((1, 2 * CAP, TOK), lambda s: (s, 0, 0)),
            spec,
            spec,
            pl.BlockSpec((1, 2 * CAP, META), lambda s: (s, 0, 0)),
        ],
        out_specs=pl.BlockSpec((1, TOK, full), lambda s: (s, 0, 0)),
        name="spread_rows",
    )(sel, yrows, dxrows, rrows)


def _bits(v):
    return lax.reduce_precision(v, 8, 7)


def on_device(tokens, routes, route_weights, cotangent, gate_proj, up_proj, down_proj):
    width = tokens.shape[1]
    hid = gate_proj.shape[2]
    me = lax.axis_index("expert")
    w_hi = _bits(route_weights)
    w_mid = _bits(route_weights - w_hi)
    w_lo = route_weights - w_hi - w_mid
    meta = jnp.concatenate(
        [routes.astype(F32), w_hi, w_mid, w_lo, jnp.zeros((TOK, META - 32), F32)], 1
    ).astype(BF)
    everything = _gather(jnp.concatenate([tokens, cotangent, meta], 1))

    meta_all = everything[:, :, 2 * width :].astype(F32)
    named = meta_all[:, :, 0:8].astype(jnp.int32)
    weights = meta_all[:, :, 8:16] + meta_all[:, :, 16:24] + meta_all[:, :, 24:32]
    mine = 2 * me + jnp.arange(2, dtype=jnp.int32)
    match = named[:, None, :, :] == mine[None, :, None, None]
    hit = jnp.any(match, axis=3)
    wtok = jnp.sum(jnp.where(match, weights[:, None], 0.0), axis=3)
    tri = (jnp.arange(TOK)[:, None] < jnp.arange(TOK)[None, :]).astype(BF)
    place = jnp.dot(hit.reshape(64, TOK).astype(BF), tri, preferred_element_type=F32)
    place = place.reshape(32, 2, 1, TOK).astype(jnp.int32)
    chosen = hit[:, :, None, :] & (place == jnp.arange(CAP, dtype=jnp.int32)[None, None, :, None])
    sel = chosen.astype(BF).reshape(32, 2 * CAP, TOK)
    wrow = jnp.sum(jnp.where(chosen, wtok[:, :, None, :], 0.0), axis=3)

    xr, cr = _pick(everything, sel, wrow.reshape(32, 2 * CAP, 1), width)
    xr = xr.reshape(2, 32 * CAP, width)
    cr = cr.reshape(2, 32 * CAP, width)
    we = jnp.transpose(wrow, (1, 0, 2)).reshape(2, 32 * CAP, 1)

    gate_pre = jnp.einsum("erd,edh->erh", xr, gate_proj, preferred_element_type=F32)
    up_pre = jnp.einsum("erd,edh->erh", xr, up_proj, preferred_element_type=F32)
    sig = jax.nn.sigmoid(gate_pre)
    swish = gate_pre * sig
    d_swish = sig * (1.0 + gate_pre * (1.0 - sig))
    hidden = (swish * up_pre).astype(BF)
    d_hidden = jnp.einsum("erd,ehd->erh", cr, down_proj, preferred_element_type=F32)
    d_gate = (d_hidden * up_pre * d_swish).astype(BF)
    d_up = (d_hidden * swish).astype(BF)
    rw = jnp.sum(d_hidden * hidden.astype(F32), axis=2, keepdims=True) / jnp.where(we > 0, we, 1.0)

    def grad(rows, cots):
        g = jnp.einsum("erd,erh->edh", rows, cots, preferred_element_type=F32).astype(BF)
        return g.reshape(2, 4, width // 4, hid)

    gg, ug, dg = grad(xr, d_gate), grad(xr, d_up), grad(cr, hidden)
    yrows = (jnp.einsum("erh,ehd->erd", hidden, down_proj, preferred_element_type=F32) * we).astype(BF)
    dxrows = (
        jnp.einsum("erh,edh->erd", d_gate, gate_proj, preferred_element_type=F32)
        + jnp.einsum("erh,edh->erd", d_up, up_proj, preferred_element_type=F32)
    ).astype(BF)
    lane = jnp.arange(META, dtype=jnp.int32)
    r_hi = _bits(rw)
    r_lo = rw - r_hi
    spot = lane[None, None, :] - mine[:, None, None]
    rrows = jnp.where(spot == 0, r_hi, 0.0) + jnp.where(spot == 64, r_lo, 0.0)
    rrows = rrows.reshape(2, 32, CAP, META).transpose(1, 0, 2, 3).reshape(32, 2 * CAP, META).astype(BF)

    part = _spread(
        sel, yrows.reshape(2, 32, CAP, width), dxrows.reshape(2, 32, CAP, width), rrows
    )
    out, go, uo, do, _ = _reduce(part, gg, ug, dg)
    table = out[:, 2 * width : 2 * width + 64].astype(F32) + out[:, 2 * width + 64 :].astype(F32)
    onehot = routes[:, :, None] == jnp.arange(64, dtype=jnp.int32)[None, None, :]
    weight_grad = jnp.sum(jnp.where(onehot, table[:, None, :], 0.0), axis=2)

    def final(g):
        return jnp.transpose(g, (1, 0, 2))

    return (out[:, :width], out[:, width : 2 * width], weight_grad, final(go), final(uo), final(do))


def solution(mesh):
    rows = P(("dp", "expert"), None)
    experts = P("expert", None, None)
    grads = P("dp", "expert", None)
    return jax.shard_map(
        on_device,
        mesh=mesh,
        in_specs=(rows, rows, rows, rows, experts, experts, experts),
        out_specs=(rows, rows, rows, grads, grads, grads),
        check_vma=False,
    )
```

time: 521 us -> 435 us (0.83)
  the two profiles are of different devices: /device:TPU:8 before, /device:TPU:1 now
where the time goes in v1:
time: 435 us; the launch traced here: 429 us
  Pallas kernels  301 us (69%)
  matrix products  92.1 us (21%)
  local copies, waits for them, and re-layouts  23.6 us (5%)
  other arithmetic  10.5 us (2%)
    pallas_call x1, Pallas kernels, _reduce(): pl.pallas_call(_reduce_kernel, out_shape=(jax.ShapeDtypeStruct((TOK, widt...  139 us
    pallas_call x1, Pallas kernels, _gather(): pl.pallas_call(_gather_kernel, out_shape=jax.ShapeDtypeStruct((32, TOK, w...  99.9 us
    pallas_call x1, Pallas kernels, _spread(): pl.pallas_call(_spread_kernel, grid=(32,), out_shape=jax.ShapeDtypeStruct...  32.5 us
    dot_general x3, matrix products, grad(): jnp.einsum('erd,erh->edh', rows, cots, preferred_element_type=F32)  31.3 us
    pallas_call x1, Pallas kernels, _pick(): pl.pallas_call(_pick_kernel, grid=(32,), out_shape=(rows, rows), in_specs...  29.8 us
    dot_general x1, matrix products, on_device(): jnp.einsum('erd,ehd->erh', cr, down_proj, preferred_element_type=F32)  14.6 us
    unnamed x28, local copies, waits for them, and re-layouts  13.3 us
    dot_general x1, matrix products, on_device(): jnp.einsum('erh,edh->erd', d_up, up_proj, preferred_element_type=F32)  10.8 us

profile of v1, /device:TPU:1, one launch (start us, length us, event | category | flops | bytes accessed | tf_op | source)
XLA Modules:
  0.0 428.7 jit_solution(10346794173426449306)
XLA Ops:
  0.7 0.1 eq.78
  0.7 0.1 fusion.11
  0.8 0.7 convert_convert_fusion
  1.5 0.7 fusion.14
  2.2 0.1 copy.119
  2.3 0.1 copy.120
  2.5 0.1 copy.118
  2.6 0.8 copy.117
  3.4 3.1 concatenate.6.blk
  6.5 99.9 %plane_gather.1.all_ref = bf16[32,128,4224]{2,1,0:T(8,128)(2,1)} custom-call(bf16[128,4224]{1,0:T(8,128)(2,1)} %concatenate.6.blk), custom_call_target="tpu_custom_call" | custom-call | tf_op jit(solution)/shard_map/plane_gather/pallas_call | solution.py:154
  106.3 1.5 slice_convert_fusion.1
  107.8 3.1 slice_add_fusion
  110.9 2.2 copy.124
  113.0 0.6 copy.121
  113.6 0.2 fusion.4
  113.8 0.2 compare_reduce_fusion
  113.9 0.1 convolution_convert_fusion.3
  114.1 0.4 select_reduce_fusion
  114.5 0.1 copy.125
  114.6 0.1 mul.36
  114.7 1.0 fusion.3.s_ref
  115.6 1.2 copy.126.w_ref
  116.9 29.8 %pick_rows.1 = (bf16[2,32,24,2048]{3,2,1,0:T(8,128)(2,1)}, bf16[2,32,24,2048]{3,2,1,0:T(8,128)(2,1)}) custom-call(bf16[32,128,4224]{2,1,0:T(8,128)(2,1)} %plane_gather.1.all_ref, bf16[32,48,128]{2,1,0:T(8,128)(2,1)} %fusion.3.s_ref, f32[32,48,1]{2,1,0:T(8,128)} %copy.126.w_ref), custom_call_target="tpu_custom_call" | custom-call | tf_op jit(solution)/shard_map/pick_rows/pallas_call | solution.py:457
  146.7 0.0 copy-start.3
  146.7 10.7 %fusion.16 = f32[2,768,640]{1,2,0:T(8,128)} fusion(bf16[2,768,2048]{2,1,0:T(8,128)(2,1)} %bitcast.71, bf16[2,2048,640]{2,1,0:T(8,128)(2,1)} %param.12), kind=kOutput, calls=%fused_computation.49 | convolution fusion | flops 4026531840 | bytes 15466496 | tf_op jit(solution)/shard_map/erd,edh->erh/dot_general | solution.py:539
  157.4 0.0 copy-done.3
  157.4 9.0 %fusion.15 = f32[2,768,640]{1,2,0:T(8,128)} fusion(bf16[2,768,2048]{2,1,0:T(8,128)(2,1)S(1)} %bitcast.74, bf16[2,2048,640]{2,1,0:T(8,128)(2,1)} %param.11), kind=kOutput, calls=%fused_computation.48 | convolution fusion | flops 4026531840 | bytes 15466496 | tf_op jit(solution)/shard_map/erd,edh->erh/dot_general | solution.py:538
  166.4 14.6 %multiply_reduce_fusion = (f32[2,768]{1,0:T(2,128)S(1)}, bf16[2,768,640]{1,2,0:T(8,128)(2,1)}, bf16[2,768,640]{1,2,0:T(8,128)(2,1)}, bf16[2,768,640]{1,2,0:T(8,128)(2,1)S(1)}) fusion(f32[2,768,640]{1,2,0:T(8,128)} %fusion.16, f32[2,768,640]{1,2,0:T(8,128)} %fusion.15, bf16[2,768,2048]{2,1,0:T(8,128)(2,1)} %bitcast.75, bf16[2,640,2048]{2,1,0:T(8,128)(2,1)} %param.13), kind=kOutput, calls=%fused_computation.5 | convolution fusion | flops 4044225024 | bytes 25303040 | tf_op jit(solution)/shard_map/erd,ehd->erh/dot_general | solution.py:544
  181.0 10.2 %convolution_convert_fusion = bf16[2,2048,640]{2,1,0:T(8,128)(2,1)} fusion(bf16[2,768,2048]{2,1,0:T(8,128)(2,1)} %bitcast.76, bf16[2,768,640]{1,2,0:T(8,128)(2,1)} %get-tuple-element.49), kind=kOutput, calls=%fused_computation.2 | convolution fusion | flops 4029153280 | bytes 13500416 | tf_op jit(solution)/shard_map/erd,erh->edh/dot_general | solution.py:550
  191.2 0.1 reduce_sum.41
  191.3 0.1 copy.134
  191.4 0.1 copy.135
  191.5 0.1 copy.136
  191.5 1.2 add_convert_fusion.1.r_ref
  192.8 0.0 slice-start
  192.8 0.0 slice-start.2
  192.8 10.3 %convolution_convert_fusion.2 = bf16[2,2048,640]{2,1,0:T(8,128)(2,1)} fusion(bf16[2,768,2048]{2,1,0:T(8,128)(2,1)} %bitcast.72, bf16[2,768,640]{1,2,0:T(8,128)(2,1)} %get-tuple-element.50), kind=kOutput, calls=%fused_computation.4 | convolution fusion | flops 4029153280 | bytes 13500416 | tf_op jit(solution)/shard_map/erd,erh->edh/dot_general | solution.py:550
  203.1 10.8 %convolution_convert_fusion.1 = bf16[2,2048,640]{2,1,0:T(8,128)(2,1)} fusion(bf16[2,768,2048]{2,1,0:T(8,128)(2,1)} %bitcast.73, bf16[2,768,640]{1,2,0:T(8,128)(2,1)S(1)} %get-tuple-element.51), kind=kOutput, calls=%fused_computation.3 | convolution fusion | flops 4029153280 | bytes 13500416 | tf_op jit(solution)/shard_map/erd,erh->edh/dot_general | solution.py:550
  213.9 0.0 slice-done
  213.9 0.0 slice-done.1
  213.9 0.0 copy-done.5
  213.9 0.0 copy-start.4
  213.9 0.0 slice-start.4
  214.0 7.0 %multiply_convert_fusion = bf16[2,768,2048]{2,1,0:T(8,128)(2,1)} fusion(f32[2,768]{1,0:T(2,128)S(1)} %mul.36, bf16[2,768,640]{1,2,0:T(8,128)(2,1)S(1)} %copy-done.5, bf16[2,640,2048]{2,1,0:T(8,128)(2,1)S(1)} %bitcast.78), kind=kOutput, calls=%fused_computation.1 | convolution fusion | flops 4032823296 | bytes 13506560 | tf_op jit(solution)/shard_map/erh,ehd->erd/dot_general | solution.py:554
  220.9 0.0 slice-done.2
  220.9 0.0 slice-done.3
  220.9 0.0 copy-done.4
  221.0 8.5 %fusion.17 = f32[2,768,2048]{2,1,0:T(8,128)} fusion(bf16[2,768,640]{1,2,0:T(8,128)(2,1)S(1)} %copy-done.4, bf16[2,2048,640]{2,1,0:T(8,128)(2,1)S(1)} %bitcast.80), kind=kOutput, calls=%fused_computation.50 | convolution fusion | flops 4026531840 | bytes 19791872 | tf_op jit(solution)/shard_map/erh,edh->erd/dot_general | solution.py:556
  229.5 0.0 slice-done.4
  229.5 0.0 slice-done.5
  229.5 10.8 %add_convert_fusion = bf16[2,768,2048]{2,1,0:T(8,128)(2,1)} fusion(f32[2,768,2048]{2,1,0:T(8,128)} %fusion.17, bf16[2,768,640]{1,2,0:T(8,128)(2,1)S(1)} %get-tuple-element.51, bf16[2,2048,640]{2,1,0:T(8,128)(2,1)S(1)} %bitcast.82), kind=kOutput, calls=%fused_computation | convolution fusion | flops 4032823296 | bytes 26083328 | tf_op jit(solution)/shard_map/erh,edh->erd/dot_general | solution.py:557
  240.3 32.5 %spread_rows.1.part = bf16[32,128,4224]{2,1,0:T(8,128)(2,1)} custom-call(bf16[32,48,128]{2,1,0:T(8,128)(2,1)} %fusion.3.s_ref, bf16[2,32,24,2048]{3,2,1,0:T(8,128)(2,1)} %bitcast.57, bf16[2,32,24,2048]{3,2,1,0:T(8,128)(2,1)} %bitcast.58, bf16[32,48,128]{2,1,0:T(8,128)(2,1)} %add_convert_fusion.1.r_ref), custom_call_target="tpu_custom_call" | custom-call | tf_op jit(solution)/shard_map/spread_rows/pallas_call | solution.py:488
  272.9 139.2 %plane_and_z_reduce.1 = (bf16[128,4224]{1,0:T(8,128)(2,1)}, f32[2,512,640]{2,1,0:T(8,128)}, f32[2,512,640]{2,1,0:T(8,128)}, f32[2,512,640]{2,1,0:T(8,128)}, bf16[2,16,64,4224]{3,2,1,0:T(8,128)(2,1)}) custom-call(bf16[32,128,4224]{2,1,0:T(8,128)(2,1)} %spread_rows.1.part, bf16[2,4,512,640]{3,2,1,0:T(8,128)(2,1)} %bitcast.60, ...), custom_call_target="tpu_custom_call" | custom-call | tf_op jit(solution)/shard_map/plane_and_z_reduce/pallas_call | solution.py:405
  412.1 0.0 copy-start.1
  412.1 5.4 %copy.144 = f32[512,2,640]{2,1,0:T(2,128)} copy(f32[512,2,640]{2,0,1:T(8,128)} %bitcast.64) | data formatting | bytes 5242880
  417.5 0.0 copy-done.1
  417.5 3.5 copy.145
  421.0 0.9 convert_add_fusion
  422.0 0.1 copy.143
  422.0 2.3 fusion.13
  424.3 0.0 copy-done.2
  424.3 0.6 select_reduce_fusion.1
  424.9 0.0 copy-done
  425.0 3.5 copy.146
  (18 shorter events, 0.1 us)
Async XLA Ops:
  146.7 10.7 %copy-start.3 = (bf16[2,32,24,2048]{3,2,1,0:T(8,128)(2,1)S(1)}, bf16[2,32,24,2048]{3,2,1,0:T(8,128)(2,1)}, u32[]{:S(2)}) copy-start(bf16[2,32,24,2048]{3,2,1,0:T(8,128)(2,1)} %get-tuple-element.12) | copy-start | bytes 18874372
  192.8 21.2 %slice-start = ((s8[5242880]{0:T(1024)(128)(4,1)}), s8[4194304]{0:T(1024)(128)(4,1)S(1)}, s32[]{:S(2)}) async-start(s8[5242880]{0:T(1024)(128)(4,1)} %bitcast.77), calls=%async_computation | async-start | bytes 8388608
  192.8 28.2 %slice-start.2 = ((s8[5242880]{0:T(1024)(128)(4,1)}), s8[4194304]{0:T(1024)(128)(4,1)S(1)}, s32[]{:S(2)}) async-start(s8[5242880]{0:T(1024)(128)(4,1)} %bitcast.79), calls=%async_computation.2 | async-start | bytes 8388608
  203.1 10.8 %slice-start.1 = ((s8[5242880]{0:T(1024)(128)(4,1)}), s8[1048576]{0:T(1024)(128)(4,1)S(1)}, s32[]{:S(2)}) async-start(s8[5242880]{0:T(1024)(128)(4,1)} %bitcast.77), calls=%async_computation.1 | async-start | bytes 2097152
  203.1 10.8 %copy-start.5 = (bf16[2,768,640]{1,2,0:T(8,128)(2,1)S(1)}, bf16[2,768,640]{1,2,0:T(8,128)(2,1)}, u32[]{:S(2)}) copy-start(bf16[2,768,640]{1,2,0:T(8,128)(2,1)} %get-tuple-element.49) | copy-start | bytes 5898244
  203.1 17.9 %slice-start.3 = ((s8[5242880]{0:T(1024)(128)(4,1)}), s8[1048576]{0:T(1024)(128)(4,1)S(1)}, s32[]{:S(2)}) async-start(s8[5242880]{0:T(1024)(128)(4,1)} %bitcast.79), calls=%async_computation.3 | async-start | bytes 2097152
  213.9 7.0 %copy-start.4 = (bf16[2,768,640]{1,2,0:T(8,128)(2,1)S(1)}, bf16[2,768,640]{1,2,0:T(8,128)(2,1)}, u32[]{:S(2)}) copy-start(bf16[2,768,640]{1,2,0:T(8,128)(2,1)} %get-tuple-element.50) | copy-start | bytes 5898244
  213.9 15.6 %slice-start.4 = ((s8[5242880]{0:T(1024)(128)(4,1)}), s8[4194304]{0:T(1024)(128)(4,1)S(1)}, s32[]{:S(2)}) async-start(s8[5242880]{0:T(1024)(128)(4,1)} %bitcast.81), calls=%async_computation.4 | async-start | bytes 8388608
  220.9 8.6 %slice-start.5 = ((s8[5242880]{0:T(1024)(128)(4,1)}), s8[1048576]{0:T(1024)(128)(4,1)S(1)}, s32[]{:S(2)}) async-start(s8[5242880]{0:T(1024)(128)(4,1)} %bitcast.81), calls=%async_computation.5 | async-start | bytes 2097152
  412.1 5.4 %copy-start.1 = (f32[2,512,640]{2,1,0:T(8,128)S(1)}, f32[2,512,640]{2,1,0:T(8,128)}, u32[]{:S(2)}) copy-start(f32[2,512,640]{2,1,0:T(8,128)} %get-tuple-element.16) | copy-start | bytes 7864324
  417.5 6.8 %copy-start.2 = (s32[128,8]{0,1:T(8,128)S(1)}, s32[128,8]{0,1:T(8,128)}, u32[]{:S(2)}) copy-start(s32[128,8]{0,1:T(8,128)} %param.8) | copy-start | bytes 12292
  417.5 7.4 %copy-start = (f32[2,512,640]{2,1,0:T(8,128)S(1)}, f32[2,512,640]{2,1,0:T(8,128)}, u32[]{:S(2)}) copy-start(f32[2,512,640]{2,1,0:T(8,128)} %get-tuple-element.17) | copy-start | bytes 7864324
